TPU v7x, 32 devices: a whole 2x2x4 slice. The times are simulated.
32 devices in a mesh: row: 4 (over z), col: 8 (over y, x, core).
Axes of the slice: x: 2, y: 2, z: 4, core: 2. Of those that a mesh axis runs over, the one named last changes fastest.
Arguments:
- embedding: float32 [4096, 256], P(('row', 'col')), may hold values from -6 to 6
- seed_cluster: int32 [4096], P(('row', 'col')), may hold values from 0 to 127
Outputs:
- log_member: float32 [4096, 128], P(('row', 'col'))
All inputs are finite; a program needn't handle non-finite values.
Results may differ from a plain program's by a relative error of at most 0.0003.
Values sent between devices are 32-bit elements; how exact they have to be, the bound alone decides.
A program may use at most 64 MiB of HBM per device.

v0:
```python
import jax
import jax.numpy as jnp
from jax import lax
from jax.sharding import PartitionSpec as P

CLUSTER_COUNT = 128
SWEEPS = 2
ANNEAL_TEMP_VALUE = 0.02


def shards(embedding, seed_cluster):
    per_device = embedding.shape[0]
    row_coords = lax.all_gather(embedding, "col", axis=0, tiled=True)
    col_coords, col_seeds = (
        lax.all_gather(embedding, "row", axis=0, tiled=True),
        lax.all_gather(seed_cluster, "row", axis=0, tiled=True),
    )
    row_sq = jnp.sum(row_coords * row_coords, axis=1)
    col_sq = jnp.sum(col_coords * col_coords, axis=1)
    inner = jnp.dot(row_coords, col_coords.T, precision=lax.Precision.HIGHEST)
    distance = jnp.sqrt(row_sq[:, None] + col_sq[None, :] - 2.0 * inner + 1.0)
    cluster_labels = jnp.arange(CLUSTER_COUNT, dtype=jnp.int32)
    member_cols = (
        0.5 * (col_seeds[:, None] == cluster_labels[None, :]).astype(jnp.float32)
        + 0.5 / CLUSTER_COUNT
    )
    member_own = (
        0.5 * (seed_cluster[:, None] == cluster_labels[None, :]).astype(jnp.float32)
        + 0.5 / CLUSTER_COUNT
    )
    log_member = jnp.zeros((per_device, CLUSTER_COUNT), jnp.float32)
    for sweep in range(SWEEPS):
        columns = member_cols
        attraction = lax.psum_scatter(
            jnp.dot(distance, columns, precision=lax.Precision.HIGHEST),
            "col",
            scatter_dimension=0,
            tiled=True,
        )
        counts, cohesion = lax.psum(
            (jnp.sum(member_own, axis=0), jnp.sum(member_own * attraction, axis=0)), ("row", "col")
        )
        pair_energy = attraction / counts[None, :] - cohesion[None, :] / (
            2.0 * counts[None, :] ** 2
        )
        member_logits = -pair_energy / ANNEAL_TEMP_VALUE
        highest = jnp.max(member_logits, axis=1, keepdims=True)
        log_member = (
            member_logits
            - highest
            - jnp.log(jnp.sum(jnp.exp(member_logits - highest), axis=1, keepdims=True))
        )
        member_own = jnp.exp(log_member)
        if sweep + 1 < SWEEPS:
            member_cols = lax.all_gather(member_own, "row", axis=0, tiled=True)
    return log_member


def solution(mesh):
    return jax.shard_map(
        shards,
        mesh=mesh,
        in_specs=(P(("row", "col"), None), P(("row", "col"))),
        out_specs=P(("row", "col"), None),
        check_vma=False,
    )
```

profile of v0, /device:TPU:0, one launch (start us, length us, event | category | flops | bytes accessed | tf_op | source)
XLA Modules:
  0.0 222.9 jit_solution(15321643899458992196)
XLA Ops:
  6.5 0.0 all-gather.3.cloned.1.call-start
  6.5 0.7 all-gather.3.cloned.1.call-update
  7.3 0.0 reduce-scatter.3.cloned.1.call-start
  7.3 12.8 %all-gather = s32[4,1,128]{2,1,0:T(1,128)S(1)} all-gather(s32[1,1,128]{2,1,0:T(1,128)} %bitcast.8), channel_id=1, replica_groups=mesh['row'=4,'col'=8] {'row'}, dimensions={0}, use_global_device_ids=true | all-gather | bytes 2560 | tf_op jit(solution)/shard_map/all_gather | solution.py:16
  20.1 15.0 %all_gather.13 = f32[512,256]{1,0:T(8,128)S(1)} all-gather(f32[128,256]{1,0:T(8,128)} %param.2), channel_id=1, replica_groups=mesh['row'=4,'col'=8] {'row'}, dimensions={0}, use_global_device_ids=true | all-gather | bytes 655360 | tf_op jit(solution)/shard_map/all_gather | solution.py:15
  35.1 0.1 multiply_reduce_fusion.1
  35.2 0.1 all-gather.3.cloned.1.call-done
  35.3 1.4 multiply_reduce_fusion
  36.8 3.9 %add_sqrt_fusion = f32[1024,512]{1,0:T(8,128)S(1)} fusion(f32[1024,256]{1,0:T(8,128)} %all-gather.3.cloned.1.call-done, f32[512,256]{1,0:T(8,128)S(1)} %all_gather.13, f32[512]{0:T(512)S(1)} %multiply_reduce_fusion.1, f32[1024]{0:T(1024)S(1)} %multiply_reduce_fusion), kind=kOutput, calls=%fused_computation | convolution fusion | flops 1612709888 | bytes 3676160 | tf_op jit(solution)/shard_map/dot_general | solution.py:20
  40.7 0.0 copy-start.1
  40.7 2.7 %fusion = f32[1024,128]{1,0:T(8,128)} fusion(f32[1024,512]{1,0:T(8,128)S(1)} %add_sqrt_fusion, s32[512]{0:T(512)S(1)} %bitcast.7), kind=kOutput, calls=%fused_computation.3 | convolution fusion | flops 805502976 | bytes 2623488 | tf_op jit(solution)/shard_map/dot_general | solution.py:35
  43.3 0.0 reduce-scatter.3.cloned.1.call-update
  43.4 0.0 reduce-scatter.5.cloned.1.call-start
  43.4 34.2 %reduce-scatter.3.cloned.1.call-done = f32[128,128]{1,0:T(8,128)} async-done(((f32[1024,128]{1,0:T(8,128)}), f32[128,128]{1,0:T(8,128)}) %reduce-scatter.3.cloned.1.call-update) | async-done | bytes 65552 | tf_op jit(solution)/shard_map/reduce_scatter | solution.py:34
  77.6 0.0 copy-done.1
  77.6 0.0 copy-start
  77.6 1.0 fusion.7
  78.7 39.3 %all-reduce.1 = (f32[128]{0:T(128)S(1)}, f32[128]{0:T(128)S(1)}) all-reduce(f32[128]{0:T(128)S(1)} %get-tuple-element.8, f32[128]{0:T(128)S(1)} %get-tuple-element.7), channel_id=1, replica_groups=mesh['row'=4,'col'=8] {'row','col'}, use_global_device_ids=true, to_apply=%region_6.0 | all-reduce | flops 256 | bytes 2048 | tf_op jit(solution)/shard_map/psum | solution.py:40
  118.0 1.0 fusion.11
  118.9 1.0 exponential_reduce_fusion.1
  120.0 1.0 subtract_exponential_fusion
  120.9 14.4 %all_gather.15 = f32[512,128]{1,0:T(8,128)S(1)} all-gather(f32[128,128]{1,0:T(8,128)S(1)} %subtract_exponential_fusion), channel_id=1, replica_groups=mesh['row'=4,'col'=8] {'row'}, dimensions={0}, use_global_device_ids=true | all-gather | bytes 327680 | tf_op jit(solution)/shard_map/all_gather | solution.py:55
  135.3 2.6 %fusion.14 = f32[1024,128]{1,0:T(8,128)} fusion(f32[1024,512]{1,0:T(8,128)S(1)} %add_sqrt_fusion, f32[512,128]{1,0:T(8,128)S(1)} %all_gather.15), kind=kOutput, calls=%fused_computation.30 | convolution fusion | flops 805306368 | bytes 2883584 | tf_op jit(solution)/shard_map/dot_general | solution.py:35
  137.9 0.0 reduce-scatter.5.cloned.1.call-update
  137.9 34.6 %reduce-scatter.5.cloned.1.call-done = f32[128,128]{1,0:T(8,128)} async-done(((f32[1024,128]{1,0:T(8,128)}), f32[128,128]{1,0:T(8,128)}) %reduce-scatter.5.cloned.1.call-update) | async-done | bytes 65552 | tf_op jit(solution)/shard_map/reduce_scatter | solution.py:34
  172.5 0.0 copy-done
  172.5 1.0 fusion.13
  173.5 39.3 %all-reduce = (f32[128]{0:T(128)S(1)}, f32[128]{0:T(128)S(1)}) all-reduce(f32[128]{0:T(128)S(1)} %get-tuple-element.6, f32[128]{0:T(128)S(1)} %get-tuple-element.5), channel_id=1, replica_groups=mesh['row'=4,'col'=8] {'row','col'}, use_global_device_ids=true, to_apply=%region_13.0 | all-reduce | flops 256 | bytes 2048 | tf_op jit(solution)/shard_map/psum | solution.py:40
  212.8 1.0 fusion.12
  213.7 1.0 exponential_reduce_fusion
  214.8 1.6 subtract_subtract_fusion
  (4 shorter events, 0.0 us)
Async XLA Ops:
  6.5 28.8 %all-gather.3.cloned.1.call-start = ((), (), s32[]{:S(2)}) async-start(), calls=%async_computation.2 | async-start | bytes 1179648 | tf_op jit(solution)/shard_map/all_gather | solution.py:13
  7.3 70.4 %reduce-scatter.3.cloned.1.call-start = ((), (), s32[]{:S(2)}) async-start(), calls=%async_computation.3 | async-start | bytes 589824 | tf_op jit(solution)/shard_map/reduce_scatter | solution.py:34
  40.7 37.0 %copy-start.1 = (s32[128]{0:T(128)S(1)}, s32[128]{0:T(128)}, u32[]{:S(2)}) copy-start(s32[128]{0:T(128)} %param.3) | copy-start | bytes 1540
  43.4 129.1 %reduce-scatter.5.cloned.1.call-start = ((), (), s32[]{:S(2)}) async-start(), calls=%async_computation.4 | async-start | bytes 589824 | tf_op jit(solution)/shard_map/reduce_scatter | solution.py:34
  77.6 94.8 %copy-start = (f32[128,128]{1,0:T(8,128)S(1)}, f32[128,128]{1,0:T(8,128)}, u32[]{:S(2)}) copy-start(f32[128,128]{1,0:T(8,128)} %reduce-scatter.3.cloned.1.call-done) | copy-start | bytes 196612
Sparse Core Ops, SparseCore 0:
  9.2 26.0 all-gather.2
  43.5 34.1 reduce-scatter.2
  138.0 34.4 reduce-scatter.4
where the time goes:
time: 224 us; the launch traced here: 223 us
  blocking collectives  121 us (54%)
  waiting for transfers between devices  69.7 us (31%)
  between operations  13.2 us (6%)
  other arithmetic  10 us (4%)
  matrix products  9.11 us (4%)
    psum x2, blocking collectives, shards(): lax.psum((jnp.sum(member_own, axis=0), jnp.sum(member_own * attraction, a...  78.6 us
    reduce_scatter x2, waiting for transfers between devices, shards(): lax.psum_scatter(jnp.dot(distance, columns, precision=lax.Precision.HIGHE...  68.8 us
    all_gather x1, blocking collectives, shards(): lax.all_gather(embedding, 'row', axis=0, tiled=True)  15 us
    all_gather x1, blocking collectives, shards(): member_cols = lax.all_gather(member_own, 'row', axis=0, tiled=True)  14.4 us
    all_gather x1, blocking collectives, shards(): lax.all_gather(seed_cluster, 'row', axis=0, tiled=True)  12.8 us
    dot_general x2, matrix products, shards(): jnp.dot(distance, columns, precision=lax.Precision.HIGHEST)  5.25 us
  transfers between devices with their start and end apart: 3, of which 3 were waited for; matrix products, arithmetic and copies ran while one was open for 0% of the time, Pallas kernels for 0%

commit v1 on v0

--- a/solution.py
+++ b/solution.py
@@ -6,6 +6,11 @@
 CLUSTER_COUNT = 128
 SWEEPS = 2
 ANNEAL_TEMP_VALUE = 0.02
+
+
+def one_after_other(x, inner_axis, outer_axis):
+    half = lax.psum(x, inner_axis)
+    return lax.psum(half, outer_axis)
 
 
 def shards(embedding, seed_cluster):
@@ -37,8 +42,8 @@
             scatter_dimension=0,
             tiled=True,
         )
-        counts, cohesion = lax.psum(
-            (jnp.sum(member_own, axis=0), jnp.sum(member_own * attraction, axis=0)), ("row", "col")
+        counts, cohesion = one_after_other(
+            (jnp.sum(member_own, axis=0), jnp.sum(member_own * attraction, axis=0)), "col", "row"
         )
         pair_energy = attraction / counts[None, :] - cohesion[None, :] / (
             2.0 * counts[None, :] ** 2

time: 224 us -> 189 us (0.84)
  blocking collectives: 121 us -> 89.2 us
  waiting for transfers between devices: 69.7 us -> 67 us
    psum x2 -> x4, blocking collectives: 78.6 us -> 47.6 us  [the longest x2 24.3 us: one_after_other(): half = lax.psum(x, inner_axis)]
    reduce_scatter x2, waiting for transfers between devices: 68.8 us -> 66.1 us  [shards(): lax.psum_scatter(jnp.dot(distance, columns, precision=lax.Precision.HIGHE...]
where the time goes in v1:
time: 189 us
  blocking collectives  89.2 us (47%)
  waiting for transfers between devices  67 us (35%)
  between operations  13.2 us (7%)
  other arithmetic  10.1 us (5%)
  matrix products  9.11 us (5%)
    reduce_scatter x2, waiting for transfers between devices, shards(): lax.psum_scatter(jnp.dot(distance, columns, precision=lax.Precision.HIGHE...  66.1 us
    psum x2, blocking collectives, one_after_other(): half = lax.psum(x, inner_axis)  24.3 us
    psum x2, blocking collectives, one_after_other(): return lax.psum(half, outer_axis)  23.3 us
    all_gather x1, blocking collectives, shards(): lax.all_gather(embedding, 'row', axis=0, tiled=True)  15 us
    all_gather x1, blocking collectives, shards(): member_cols = lax.all_gather(member_own, 'row', axis=0, tiled=True)  13.8 us
    all_gather x1, blocking collectives, shards(): lax.all_gather(seed_cluster, 'row', axis=0, tiled=True)  12.8 us
    dot_general x2, matrix products, shards(): jnp.dot(distance, columns, precision=lax.Precision.HIGHEST)  5.25 us
    dot_general x1, matrix products, shards(): inner = jnp.dot(row_coords, col_coords.T, precision=lax.Precision.HIGHEST)  3.86 us
  transfers between devices with their start and end apart: 3, of which 3 were waited for; matrix products, arithmetic and copies ran while one was open for 0% of the time, Pallas kernels for 0%

profile of v1, /device:TPU:0, one launch (start us, length us, event | category | flops | bytes accessed | tf_op | source)
XLA Modules:
  0.0 188.6 jit_solution(1975111163236927728)
XLA Ops:
  6.5 0.0 all-gather.3.cloned.1.call-start
  6.5 0.7 all-gather.3.cloned.1.call-update
  7.3 0.0 reduce-scatter.3.cloned.1.call-start
  7.3 12.8 %all-gather = s32[4,1,128]{2,1,0:T(1,128)S(1)} all-gather(s32[1,1,128]{2,1,0:T(1,128)} %bitcast.8), channel_id=1, replica_groups=mesh['row'=4,'col'=8] {'row'}, dimensions={0}, use_global_device_ids=true | all-gather | bytes 2560 | tf_op jit(solution)/shard_map/all_gather | solution.py:21
  20.1 15.0 %all_gather.13 = f32[512,256]{1,0:T(8,128)S(1)} all-gather(f32[128,256]{1,0:T(8,128)} %param.2), channel_id=1, replica_groups=mesh['row'=4,'col'=8] {'row'}, dimensions={0}, use_global_device_ids=true | all-gather | bytes 655360 | tf_op jit(solution)/shard_map/all_gather | solution.py:20
  35.1 0.1 multiply_reduce_fusion.1
  35.2 0.1 all-gather.3.cloned.1.call-done
  35.3 1.4 multiply_reduce_fusion
  36.8 3.9 %add_sqrt_fusion = f32[1024,512]{1,0:T(8,128)S(1)} fusion(f32[1024,256]{1,0:T(8,128)} %all-gather.3.cloned.1.call-done, f32[512,256]{1,0:T(8,128)S(1)} %all_gather.13, f32[512]{0:T(512)S(1)} %multiply_reduce_fusion.1, f32[1024]{0:T(1024)S(1)} %multiply_reduce_fusion), kind=kOutput, calls=%fused_computation | convolution fusion | flops 1612709888 | bytes 3676160 | tf_op jit(solution)/shard_map/dot_general | solution.py:25
  40.7 0.0 copy-start.1
  40.7 2.7 %fusion = f32[1024,128]{1,0:T(8,128)} fusion(f32[1024,512]{1,0:T(8,128)S(1)} %add_sqrt_fusion, s32[512]{0:T(512)S(1)} %bitcast.7), kind=kOutput, calls=%fused_computation.3 | convolution fusion | flops 805502976 | bytes 2623488 | tf_op jit(solution)/shard_map/dot_general | solution.py:40
  43.3 0.0 reduce-scatter.3.cloned.1.call-update
  43.4 0.0 reduce-scatter.5.cloned.1.call-start
  43.4 34.2 %reduce-scatter.3.cloned.1.call-done = f32[128,128]{1,0:T(8,128)} async-done(((f32[1024,128]{1,0:T(8,128)}), f32[128,128]{1,0:T(8,128)}) %reduce-scatter.3.cloned.1.call-update) | async-done | bytes 65552 | tf_op jit(solution)/shard_map/reduce_scatter | solution.py:39
  77.6 0.0 copy-done.1
  77.6 1.0 fusion.7
  78.7 12.2 %all-reduce.1 = (f32[128]{0:T(128)S(1)}, f32[128]{0:T(128)S(1)}) all-reduce(f32[128]{0:T(128)S(1)} %get-tuple-element.8, f32[128]{0:T(128)S(1)} %get-tuple-element.7), channel_id=1, replica_groups=mesh['row'=4,'col'=8] {'col'}, use_global_device_ids=true, to_apply=%region_7.0 | all-reduce | flops 256 | bytes 2048 | tf_op jit(solution)/shard_map/psum | solution.py:12
  90.8 11.7 %all-reduce.3 = (f32[128]{0:T(128)S(1)}, f32[128]{0:T(128)S(1)}) all-reduce(f32[128]{0:T(128)S(1)} %get-tuple-element.11, f32[128]{0:T(128)S(1)} %get-tuple-element.12), channel_id=1, replica_groups=mesh['row'=4,'col'=8] {'row'}, use_global_device_ids=true, to_apply=%region_8.0 | all-reduce | flops 256 | bytes 2048 | tf_op jit(solution)/shard_map/psum | solution.py:13
  102.5 1.0 fusion.11
  103.4 1.0 exponential_reduce_fusion.1
  104.5 1.0 subtract_exponential_fusion
  105.4 13.8 %all_gather.15 = f32[512,128]{1,0:T(8,128)S(1)} all-gather(f32[128,128]{1,0:T(8,128)S(1)} %subtract_exponential_fusion), channel_id=1, replica_groups=mesh['row'=4,'col'=8] {'row'}, dimensions={0}, use_global_device_ids=true | all-gather | bytes 327680 | tf_op jit(solution)/shard_map/all_gather | solution.py:60
  119.2 2.6 %fusion.14 = f32[1024,128]{1,0:T(8,128)} fusion(f32[1024,512]{1,0:T(8,128)S(1)} %add_sqrt_fusion, f32[512,128]{1,0:T(8,128)S(1)} %all_gather.15), kind=kOutput, calls=%fused_computation.30 | convolution fusion | flops 805306368 | bytes 2883584 | tf_op jit(solution)/shard_map/dot_general | solution.py:40
  121.8 0.0 reduce-scatter.5.cloned.1.call-update
  121.9 31.9 %reduce-scatter.5.cloned.1.call-done = f32[128,128]{1,0:T(8,128)} async-done(((f32[1024,128]{1,0:T(8,128)}), f32[128,128]{1,0:T(8,128)}) %reduce-scatter.5.cloned.1.call-update) | async-done | bytes 65552 | tf_op jit(solution)/shard_map/reduce_scatter | solution.py:39
  153.8 0.0 copy-done
  153.8 1.0 fusion.13
  154.7 12.1 %all-reduce = (f32[128]{0:T(128)S(1)}, f32[128]{0:T(128)S(1)}) all-reduce(f32[128]{0:T(128)S(1)} %get-tuple-element.6, f32[128]{0:T(128)S(1)} %get-tuple-element.5), channel_id=1, replica_groups=mesh['row'=4,'col'=8] {'col'}, use_global_device_ids=true, to_apply=%region_16.0 | all-reduce | flops 256 | bytes 2048 | tf_op jit(solution)/shard_map/psum | solution.py:12
  166.9 11.7 %all-reduce.2 = (f32[128]{0:T(128)S(1)}, f32[128]{0:T(128)S(1)}) all-reduce(f32[128]{0:T(128)S(1)} %get-tuple-element.9, f32[128]{0:T(128)S(1)} %get-tuple-element.10), channel_id=1, replica_groups=mesh['row'=4,'col'=8] {'row'}, use_global_device_ids=true, to_apply=%region_17.0 | all-reduce | flops 256 | bytes 2048 | tf_op jit(solution)/shard_map/psum | solution.py:13
  178.5 1.0 fusion.12
  179.5 1.0 exponential_reduce_fusion
  180.5 1.6 subtract_subtract_fusion
  (5 shorter events, 0.0 us)
Async XLA Ops:
  6.5 28.8 %all-gather.3.cloned.1.call-start = ((), (), s32[]{:S(2)}) async-start(), calls=%async_computation.2 | async-start | bytes 1179648 | tf_op jit(solution)/shard_map/all_gather | solution.py:18
  7.3 70.4 %reduce-scatter.3.cloned.1.call-start = ((), (), s32[]{:S(2)}) async-start(), calls=%async_computation.3 | async-start | bytes 589824 | tf_op jit(solution)/shard_map/reduce_scatter | solution.py:39
  40.7 37.0 %copy-start.1 = (s32[128]{0:T(128)S(1)}, s32[128]{0:T(128)}, u32[]{:S(2)}) copy-start(s32[128]{0:T(128)} %param.3) | copy-start | bytes 1540
  43.4 110.4 %reduce-scatter.5.cloned.1.call-start = ((), (), s32[]{:S(2)}) async-start(), calls=%async_computation.4 | async-start | bytes 589824 | tf_op jit(solution)/shard_map/reduce_scatter | solution.py:39
  77.6 76.1 %copy-start = (f32[128,128]{1,0:T(8,128)S(1)}, f32[128,128]{1,0:T(8,128)}, u32[]{:S(2)}) copy-start(f32[128,128]{1,0:T(8,128)} %reduce-scatter.3.cloned.1.call-done) | copy-start | bytes 196612
Sparse Core Ops, SparseCore 0:
  9.2 26.0 all-gather.2
  43.5 34.1 reduce-scatter.2
  122.0 31.7 reduce-scatter.4
